TPU v7x, 256 devices: a whole 4x4x8 slice. The times are simulated.
256 devices in a mesh: rows: 8 (over x, core), protos: 32 (over y, z).
Axes of the slice: x: 4, y: 4, z: 8, core: 2. Of those that a mesh axis runs over, the one named last changes fastest.
Arguments:
- teacher_features: bfloat16 [4096, 384], P(('rows', 'protos')), may hold values from -80 to 80, as said below
- student_features: bfloat16 [4096, 384], P(('rows', 'protos')), may hold values from -80 to 80, as said below
- prototypes: bfloat16 [131072, 384], P('protos'), may hold values from -80 to 80, as said below
Outputs:
- feature_grad: float32 [4096, 384], P(('rows', 'protos'))
- proto_grad: float32 [8, 16384, 384], P('rows', 'protos')
Inputs may be any that keep to these rules, and one draw needn't show every extreme that they name: `teacher_features`: every row has nonzero entries. `student_features`: every row has nonzero entries. `prototypes`: every row has nonzero entries.
All inputs are finite; a program needn't handle non-finite values.
Results may differ from a plain program's by a relative error of at most 0.012.
The roundings to bfloat16 on the way count: a program that leaves them out, or rounds other values in their place, can miss the bound.
Values may be sent and summed in bfloat16 or wider, within the bound.
A program may use at most 64 MiB of HBM per device.

v0:
```python
import math
import jax
import jax.numpy as jnp
from jax import lax
from jax.sharding import PartitionSpec as P

D = 384
K = 131072
PASSES = 3
eps = 1e-06


def unitize(values):
    values = values.astype(jnp.float32)
    return (values * lax.rsqrt(jnp.sum(values * values, axis=1, keepdims=True) + eps)).astype(
        jnp.bfloat16
    )


def against(left, right):
    return lax.dot_general(
        left, right, (((1,), (1,)), ((), ())), preferred_element_type=jnp.float32
    )


def on_device(teacher_features, student_features, prototypes):
    scale = 1.5 * math.sqrt(D)
    unit_w = unitize(prototypes)
    local_t = unitize(teacher_features)
    local_s = unitize(student_features)
    unit_t, unit_s = (
        lax.all_gather(local_t, "protos", axis=0, tiled=True),
        lax.all_gather(local_s, "protos", axis=0, tiled=True),
    )
    kernel = jnp.exp(scale * against(unit_t, unit_w))
    powers = jnp.exp(scale * against(unit_s, unit_w))
    student_part = jnp.sum(powers, axis=1)
    student_whole = lax.psum(student_part, "protos")
    row_scale = jnp.ones((kernel.shape[0],), jnp.float32)
    col_scale = jnp.ones((kernel.shape[1],), jnp.float32)
    for step in range(PASSES):
        col_part = jnp.dot(row_scale, kernel, precision=lax.Precision.HIGHEST)
        col_scale = 1.0 / lax.psum(col_part, "rows")
        row_part = jnp.dot(kernel, col_scale, precision=lax.Precision.HIGHEST)
        if step == 0:
            row_whole = lax.psum(row_part, "protos")
        else:
            row_whole = lax.psum(row_part, "protos")
        row_scale = 1.0 / row_whole
    target = kernel * row_scale[:, None] * col_scale[None, :]
    probs = powers / student_whole[:, None]
    delta = (probs - target).astype(jnp.bfloat16)
    feature_term = scale * jnp.dot(delta, unit_w, preferred_element_type=jnp.float32)
    feature_grad = lax.psum_scatter(feature_term, "protos", scatter_dimension=0, tiled=True)
    row_groups = lax.axis_size("rows")
    total_rows = delta.shape[0] * row_groups
    factor = scale * K / total_rows
    block = delta.shape[1] // row_groups
    term = factor * lax.dot_general(
        delta, unit_s, (((0,), (0,)), ((), ())), preferred_element_type=jnp.float32
    )
    proto_grad = lax.psum_scatter(
        term.reshape(row_groups, block, term.shape[1]), "rows", scatter_dimension=0, tiled=True
    )
    return (feature_grad, proto_grad)


def solution(mesh):
    return jax.shard_map(
        on_device,
        mesh=mesh,
        in_specs=(P(("rows", "protos"), None), P(("rows", "protos"), None), P("protos", None)),
        out_specs=(P(("rows", "protos"), None), P("rows", "protos", None)),
        check_vma=False,
    )
```

profile of v0, /device:TPU:1, one launch (start us, length us, event | category | flops | bytes accessed | tf_op | source)
XLA Modules:
  0.0 735.6 jit_solution(5828482277272511359)
XLA Ops:
  7.2 0.0 reduce-scatter.3.cloned.1.call-start
  7.2 0.8 fusion.5
  8.0 0.8 fusion.3
  8.9 0.8 fusion.4
  9.7 0.8 fusion.6
  10.4 2.6 fusion.1
  13.1 41.6 %all_gather.6 = bf16[512,384]{1,0:T(8,128)(2,1)S(1)} all-gather(bf16[16,384]{1,0:T(8,128)(2,1)S(1)} %fusion.4), channel_id=1, replica_groups=mesh['rows'=8,'protos'=32] {'protos'}, dimensions={0}, use_global_device_ids=true | all-gather | bytes 405504 | tf_op jit(solution)/shard_map/all_gather | solution.py:33
  54.6 36.7 %all_gather.7 = bf16[512,384]{1,0:T(8,128)(2,1)S(1)} all-gather(bf16[16,384]{1,0:T(8,128)(2,1)S(1)} %fusion.6), channel_id=1, replica_groups=mesh['rows'=8,'protos'=32] {'protos'}, dimensions={0}, use_global_device_ids=true | all-gather | bytes 405504 | tf_op jit(solution)/shard_map/all_gather | solution.py:32
  91.3 4.3 multiply_exponential_fusion
  95.7 3.2 copy-done
  98.9 4.0 fusion.7
  102.9 44.7 %psum.50 = f32[4096]{0:T(1024)S(1)} all-reduce(f32[4096]{0:T(1024)S(1)} %bitcast.34), channel_id=1, replica_groups=mesh['rows'=8,'protos'=32] {'rows'}, use_global_device_ids=true, to_apply=%region_5.0 | all-reduce | flops 4096 | bytes 32768 | tf_op jit(solution)/shard_map/psum | solution.py:43
  147.7 9.4 %fusion.14 = f32[1,512]{1,0:T(1,128)S(1)} fusion(f32[512,4096]{1,0:T(8,128)} %copy-done, f32[4096,1]{0,1:T(1,128)S(1)} %bitcast.30), kind=kOutput, calls=%fused_computation.31 | convolution fusion | flops 25165824 | bytes 8407040 | tf_op jit(solution)/shard_map/dot_general | solution.py:44
  157.1 58.6 %psum.51 = f32[512]{0:T(512)S(1)} all-reduce(f32[512]{0:T(512)S(1)} %bitcast.36), channel_id=1, replica_groups=mesh['rows'=8,'protos'=32] {'protos'}, use_global_device_ids=true, to_apply=%region_6.0 | all-reduce | flops 512 | bytes 4096 | tf_op jit(solution)/shard_map/psum | solution.py:46
  215.7 6.3 fusion.15
  222.1 37.4 %psum.52 = f32[4096]{0:T(1024)S(1)} all-reduce(f32[4096]{0:T(1024)S(1)} %bitcast.31), channel_id=1, replica_groups=mesh['rows'=8,'protos'=32] {'rows'}, use_global_device_ids=true, to_apply=%region_7.0 | all-reduce | flops 4096 | bytes 32768 | tf_op jit(solution)/shard_map/psum | solution.py:43
  259.5 9.4 %fusion.16 = f32[1,512]{1,0:T(1,128)S(1)} fusion(f32[512,4096]{1,0:T(8,128)} %copy-done, f32[4096,1]{0,1:T(1,128)S(1)} %bitcast.32), kind=kOutput, calls=%fused_computation.33 | convolution fusion | flops 25165824 | bytes 8407040 | tf_op jit(solution)/shard_map/dot_general | solution.py:44
  268.9 55.8 %psum.53 = f32[512]{0:T(512)S(1)} all-reduce(f32[512]{0:T(512)S(1)} %bitcast.38), channel_id=1, replica_groups=mesh['rows'=8,'protos'=32] {'protos'}, use_global_device_ids=true, to_apply=%region_8.0 | all-reduce | flops 512 | bytes 4096 | tf_op jit(solution)/shard_map/psum | solution.py:48
  324.7 6.5 fusion.17
  331.2 37.6 %psum.54 = f32[4096]{0:T(1024)} all-reduce(f32[4096]{0:T(1024)S(1)} %bitcast.33), channel_id=1, replica_groups=mesh['rows'=8,'protos'=32] {'rows'}, use_global_device_ids=true, to_apply=%region_9.0 | all-reduce | flops 4096 | bytes 32768 | tf_op jit(solution)/shard_map/psum | solution.py:43
  368.8 0.7 broadcast_divide_fusion
  369.6 10.0 %fusion.18 = f32[1,512]{1,0:T(1,128)} fusion(f32[512,4096]{1,0:T(8,128)} %copy-done, f32[4096,1]{0,1:T(1,128)S(1)} %bitcast.29), kind=kOutput, calls=%fused_computation.35 | convolution fusion | flops 25165824 | bytes 8407040 | tf_op jit(solution)/shard_map/dot_general | solution.py:44
  379.6 6.2 fusion
  385.8 58.2 %all-reduce = (f32[512]{0:T(512)}, f32[512]{0:T(512)}) all-reduce(f32[512]{0:T(512)} %bitcast.35, f32[512]{0:T(512)} %get-tuple-element.4), channel_id=1, replica_groups=mesh['rows'=8,'protos'=32] {'protos'}, use_global_device_ids=true, to_apply=%region_10.0 | all-reduce | flops 1024 | bytes 8192 | tf_op jit(solution)/shard_map/psum | solution.py:48
  444.0 0.7 broadcast_divide_fusion.5
  444.6 7.3 subtract_convert_fusion
  452.0 2.0 copy-done.2
  454.0 3.3 convolution_multiply_fusion.1
  457.4 0.0 reduce-scatter.5.cloned.1.call-start
  457.4 7.2 convolution_multiply_fusion
  464.7 212.9 %reduce-scatter.3.cloned.1.call-done = f32[16,384]{1,0:T(8,128)} async-done(((f32[512,384]{1,0:T(8,128)}), f32[16,384]{1,0:T(8,128)}) %reduce-scatter.3.cloned.1.call-update) | async-done | bytes 24592 | tf_op jit(solution)/shard_map/reduce_scatter | solution.py:54
  677.6 51.2 %reduce-scatter.5.cloned.1.call-done = f32[1,512,384]{2,1,0:T(8,128)} async-done(((f32[8,512,384]{2,1,0:T(8,128)}), f32[1,512,384]{2,1,0:T(8,128)}) %reduce-scatter.5.cloned.1.call-update) | async-done | bytes 786448 | tf_op jit(solution)/shard_map/reduce_scatter | solution.py:62
  (17 shorter events, 0.1 us)
Async XLA Ops:
  7.2 670.4 %reduce-scatter.3.cloned.1.call-start = ((), (), s32[]{:S(2)}) async-start(), calls=%async_computation.2 | async-start | bytes 811008 | tf_op jit(solution)/shard_map/reduce_scatter | solution.py:54
  13.0 89.9 %copy-start.3 = (f32[4096]{0:T(1024)}, f32[4096]{0:T(1024)S(1)}, u32[]{:S(2)}) copy-start(f32[4096]{0:T(1024)S(1)} %add_rsqrt_fusion) | copy-start | bytes 49156
  95.7 3.2 copy-start
  324.7 54.9 %copy-start.1 = (bf16[4096,384]{1,0:T(8,128)(2,1)S(1)}, bf16[4096,384]{1,0:T(8,128)(2,1)}, u32[]{:S(2)}) copy-start(bf16[4096,384]{1,0:T(8,128)(2,1)} %param.5) | copy-start | bytes 9437188
  444.6 9.4 %copy-start.4 = (f32[4096]{0:T(1024)S(1)}, f32[4096]{0:T(1024)}, u32[]{:S(2)}) copy-start(f32[4096]{0:T(1024)} %copy-done.3) | copy-start | bytes 49156
  452.0 2.0 copy-start.2
  457.4 271.4 %reduce-scatter.5.cloned.1.call-start = ((), (), s32[]{:S(2)}) async-start(), calls=%async_computation.3 | async-start | bytes 7077888 | tf_op jit(solution)/shard_map/reduce_scatter | solution.py:62
Sparse Core Ops, SparseCore 0:
  457.5 220.0 reduce-scatter.2
  680.7 48.0 reduce-scatter.4
where the time goes:
time: 736 us
  blocking collectives  371 us (50%)
  waiting for transfers between devices  264 us (36%)
  matrix products  66.9 us (9%)
  other arithmetic  14.6 us (2%)
  between operations  14.1 us (2%)
    reduce_scatter x1, waiting for transfers between devices, on_device(): lax.psum_scatter(feature_term, 'protos', scatter_dimension=0, tiled=True)  213 us
    psum x3, blocking collectives, on_device(): row_whole = lax.psum(row_part, 'protos')  173 us
    psum x3, blocking collectives, on_device(): col_scale = 1.0 / lax.psum(col_part, 'rows')  120 us
    reduce_scatter x1, waiting for transfers between devices, on_device(): lax.psum_scatter(term.reshape(row_groups, block, term.shape[1]), 'rows',...  51.2 us
    all_gather x1, blocking collectives, on_device(): lax.all_gather(local_s, 'protos', axis=0, tiled=True)  41.6 us
    all_gather x1, blocking collectives, on_device(): lax.all_gather(local_t, 'protos', axis=0, tiled=True)  36.7 us
    dot_general x3, matrix products, on_device(): row_part = jnp.dot(kernel, col_scale, precision=lax.Precision.HIGHEST)  28.9 us
    dot_general x3, matrix products, on_device(): col_part = jnp.dot(row_scale, kernel, precision=lax.Precision.HIGHEST)  16.9 us
  transfers between devices with their start and end apart: 2, of which 2 were waited for; matrix products, arithmetic and copies ran while one was open for 1% of the time, Pallas kernels for 0%

commit v1 on v0

--- a/solution.py
+++ b/solution.py
@@ -28,9 +28,26 @@
     unit_w = unitize(prototypes)
     local_t = unitize(teacher_features)
     local_s = unitize(student_features)
+
+    def number_rows(obj, link_axis):
+        r2 = lax.axis_size(link_axis)
+        val = lax.axis_index(link_axis)
+        piece_out, plain = (r2, val)
+        even, main = (obj, 1)
+        while main < piece_out:
+            crops = []
+            for src_i in range(piece_out):
+                crops.append((src_i, src_i ^ main))
+            lower = lax.ppermute(even, axis_name=link_axis, perm=crops)
+            s_next = jnp.concatenate([even, lower], axis=0)
+            w_next = jnp.concatenate([lower, even], axis=0)
+            even = jnp.where(plain & main == 0, s_next, w_next)
+            main = 2 * main
+        return even
+
     unit_t, unit_s = (
         lax.all_gather(local_t, "protos", axis=0, tiled=True),
-        lax.all_gather(local_s, "protos", axis=0, tiled=True),
+        number_rows(local_s, "protos"),
     )
     kernel = jnp.exp(scale * against(unit_t, unit_w))
     powers = jnp.exp(scale * against(unit_s, unit_w))

time: 736 us -> 700 us (0.951)
  blocking collectives: 371 us -> 324 us
  waiting for transfers between devices: 264 us -> 272 us
    all_gather x1 -> x0, blocking collectives: 41.6 us -> none  [on_device(): lax.all_gather(local_s, 'protos', axis=0, tiled=True)]
    psum x3, blocking collectives: 120 us -> 109 us  [on_device(): col_scale = 1.0 / lax.psum(col_part, 'rows')]
  transfers between devices with their start and end apart: 2 -> 7, of which waited for: 2 -> 4; matrix products, arithmetic and copies ran while one was open for 1% -> 9% of each run, Pallas kernels for 0% -> 0%
where the time goes in v1:
time: 700 us
  blocking collectives  324 us (46%)
  waiting for transfers between devices  272 us (39%)
  matrix products  66.1 us (9%)
  between operations  14.2 us (2%)
  other arithmetic  13.2 us (2%)
    reduce_scatter x1, waiting for transfers between devices, on_device(): lax.psum_scatter(feature_term, 'protos', scatter_dimension=0, tiled=True)  214 us
    psum x3, blocking collectives, on_device(): row_whole = lax.psum(row_part, 'protos')  175 us
    psum x3, blocking collectives, on_device(): col_scale = 1.0 / lax.psum(col_part, 'rows')  109 us
    reduce_scatter x1, waiting for transfers between devices, on_device(): lax.psum_scatter(term.reshape(row_groups, block, term.shape[1]), 'rows',...  51.1 us
    all_gather x1, blocking collectives, on_device(): lax.all_gather(local_t, 'protos', axis=0, tiled=True)  39.9 us
    dot_general x3, matrix products, on_device(): row_part = jnp.dot(kernel, col_scale, precision=lax.Precision.HIGHEST)  28.3 us
    dot_general x3, matrix products, on_device(): col_part = jnp.dot(row_scale, kernel, precision=lax.Precision.HIGHEST)  16.9 us
  transfers between devices with their start and end apart: 7, of which 4 were waited for; matrix products, arithmetic and copies ran while one was open for 9% of the time, Pallas kernels for 0%

profile of v1, /device:TPU:1, one launch (start us, length us, event | category | flops | bytes accessed | tf_op | source)
XLA Modules:
  0.0 699.7 jit_solution(5473202222314105378)
XLA Ops:
  7.2 0.8 fusion.4
  8.0 0.8 fusion.5
  8.8 2.5 collective-permute-start
  11.3 0.8 fusion.6
  12.1 0.8 fusion.7
  12.9 2.6 fusion.1
  15.5 39.9 %all_gather.3 = bf16[512,384]{1,0:T(8,128)(2,1)S(1)} all-gather(bf16[16,384]{1,0:T(8,128)(2,1)S(1)} %fusion.7), channel_id=1, replica_groups=mesh['rows'=8,'protos'=32] {'protos'}, dimensions={0}, use_global_device_ids=true | all-gather | bytes 405504 | tf_op jit(solution)/shard_map/all_gather | solution.py:49
  55.4 4.3 multiply_exponential_fusion
  59.8 3.2 copy-done
  63.0 4.0 fusion.8
  67.0 33.2 %psum.50 = f32[4096]{0:T(1024)S(1)} all-reduce(f32[4096]{0:T(1024)S(1)} %bitcast.32), channel_id=1, replica_groups=mesh['rows'=8,'protos'=32] {'rows'}, use_global_device_ids=true, to_apply=%region_5.6 | all-reduce | flops 4096 | bytes 32768 | tf_op jit(solution)/shard_map/psum | solution.py:60
  100.2 9.4 %fusion.16 = f32[1,512]{1,0:T(1,128)S(1)} fusion(f32[512,4096]{1,0:T(8,128)} %copy-done, f32[4096,1]{0,1:T(1,128)S(1)} %bitcast.29), kind=kOutput, calls=%fused_computation.38 | convolution fusion | flops 25165824 | bytes 8407040 | tf_op jit(solution)/shard_map/dot_general | solution.py:61
  109.7 58.6 %psum.51 = f32[512]{0:T(512)S(1)} all-reduce(f32[512]{0:T(512)S(1)} %bitcast.36), channel_id=1, replica_groups=mesh['rows'=8,'protos'=32] {'protos'}, use_global_device_ids=true, to_apply=%region_6.7 | all-reduce | flops 512 | bytes 4096 | tf_op jit(solution)/shard_map/psum | solution.py:63
  168.3 6.3 fusion.17
  174.6 37.4 %psum.52 = f32[4096]{0:T(1024)S(1)} all-reduce(f32[4096]{0:T(1024)S(1)} %bitcast.30), channel_id=1, replica_groups=mesh['rows'=8,'protos'=32] {'rows'}, use_global_device_ids=true, to_apply=%region_7.8 | all-reduce | flops 4096 | bytes 32768 | tf_op jit(solution)/shard_map/psum | solution.py:60
  212.0 9.4 %fusion.18 = f32[1,512]{1,0:T(1,128)S(1)} fusion(f32[512,4096]{1,0:T(8,128)} %copy-done, f32[4096,1]{0,1:T(1,128)S(1)} %bitcast.31), kind=kOutput, calls=%fused_computation.40 | convolution fusion | flops 25165824 | bytes 8407040 | tf_op jit(solution)/shard_map/dot_general | solution.py:61
  221.5 55.8 %psum.53 = f32[512]{0:T(512)S(1)} all-reduce(f32[512]{0:T(512)S(1)} %bitcast.35), channel_id=1, replica_groups=mesh['rows'=8,'protos'=32] {'protos'}, use_global_device_ids=true, to_apply=%region_8.9 | all-reduce | flops 512 | bytes 4096 | tf_op jit(solution)/shard_map/psum | solution.py:65
  277.4 3.5 collective-permute-done.1
  280.9 0.1 collective-permute-start.2
  281.0 6.5 fusion.19
  287.5 38.6 %psum.54 = f32[4096]{0:T(1024)S(1)} all-reduce(f32[4096]{0:T(1024)S(1)} %bitcast.28), channel_id=1, replica_groups=mesh['rows'=8,'protos'=32] {'rows'}, use_global_device_ids=true, to_apply=%region_9.10 | all-reduce | flops 4096 | bytes 32768 | tf_op jit(solution)/shard_map/psum | solution.py:60
  326.3 3.4 collective-permute-done.3
  329.7 1.2 collective-permute-start.4
  330.9 9.4 %fusion.20 = f32[1,512]{1,0:T(1,128)S(1)} fusion(f32[512,4096]{1,0:T(8,128)} %copy-done, f32[4096,1]{0,1:T(1,128)S(1)} %bitcast.27), kind=kOutput, calls=%fused_computation.42 | convolution fusion | flops 25165824 | bytes 8407040 | tf_op jit(solution)/shard_map/dot_general | solution.py:61
  340.4 6.0 fusion
  346.3 61.0 %all-reduce = (f32[512]{0:T(512)S(1)}, f32[512]{0:T(512)S(1)}) all-reduce(f32[512]{0:T(512)S(1)} %bitcast.34, f32[512]{0:T(512)S(1)} %get-tuple-element.4), channel_id=1, replica_groups=mesh['rows'=8,'protos'=32] {'protos'}, use_global_device_ids=true, to_apply=%region_10.11 | all-reduce | flops 1024 | bytes 8192 | tf_op jit(solution)/shard_map/psum | solution.py:65
  407.4 7.3 %subtract_convert_fusion = bf16[512,4096]{1,0:T(8,128)(2,1)S(1)} fusion(f32[512,4096]{1,0:T(8,128)} %copy-done, f32[512,4096]{1,0:T(8,128)} %get-tuple-element.5, f32[4096]{0:T(1024)S(1)} %broadcast_divide_fusion, f32[512]{0:T(512)S(1)} %broadcast_divide_fusion.5, f32[512]{0:T(512)S(1)} %get-tuple-element.3), kind=kLoop, calls=%fused_computation | loop fusion | flops 12582912 | bytes 20992000 | tf_op jit(solution)/shard_map/convert_element_type | solution.py:69
  414.7 2.0 copy-done.2
  416.7 3.3 convolution_multiply_fusion.1
  420.1 7.3 %convolution_multiply_fusion = f32[4096,384]{1,0:T(8,128)} fusion(bf16[512,4096]{1,0:T(8,128)(2,1)} %copy-done.2, bf16[256,384]{1,0:T(8,128)(2,1)} %collective-permute-done.4, bf16[256,384]{1,0:T(8,128)(2,1)S(1)} %maximum_select_fusion.1, pred[]{:T(512)S(6)} %eq.15), kind=kOutput, calls=%fused_computation.8 | convolution fusion | flops 1613955072 | bytes 10878977 | tf_op jit(solution)/shard_map/dot_general | solution.py:76
  427.4 214.3 %reduce-scatter.3.cloned.1.call-done = f32[16,384]{1,0:T(8,128)} async-done(((f32[512,384]{1,0:T(8,128)}), f32[16,384]{1,0:T(8,128)}) %reduce-scatter.3.cloned.1.call-update) | async-done | bytes 24592 | tf_op jit(solution)/shard_map/reduce_scatter | solution.py:71
  641.8 51.1 %reduce-scatter.5.cloned.1.call-done = f32[1,512,384]{2,1,0:T(8,128)} async-done(((f32[8,512,384]{2,1,0:T(8,128)}), f32[1,512,384]{2,1,0:T(8,128)}) %reduce-scatter.5.cloned.1.call-update) | async-done | bytes 786448 | tf_op jit(solution)/shard_map/reduce_scatter | solution.py:79
  (30 shorter events, 0.5 us)
Async XLA Ops:
  7.2 634.6 %reduce-scatter.3.cloned.1.call-start = ((), (), s32[]{:S(2)}) async-start(), calls=%async_computation.2 | async-start | bytes 811008 | tf_op jit(solution)/shard_map/reduce_scatter | solution.py:71
  8.8 268.4 %collective-permute-start = (bf16[16,384]{1,0:T(8,128)(2,1)S(1)}, bf16[16,384]{1,0:T(8,128)(2,1)S(1)}, u32[]{:S(2)}, u32[]{:S(2)}) collective-permute-start(bf16[16,384]{1,0:T(8,128)(2,1)S(1)} %fusion.5), channel_id=1, source_target_pairs={{0,1},{1,0},{2,3},{3,2},{4,5},{5,4},{6,7},{7,6},{8,9},{9,8},{10,11... | collective-permute-start | bytes 36872 | tf_op jit(solution)/shard_map/ppermute | solution.py:41
  15.5 51.5 %copy-start.3 = (f32[4096]{0:T(1024)}, f32[4096]{0:T(1024)S(1)}, u32[]{:S(2)}) copy-start(f32[4096]{0:T(1024)S(1)} %add_rsqrt_fusion) | copy-start | bytes 49156
  59.8 3.2 copy-start
  277.2 3.7 collective-permute-start.1
  280.9 45.2 %collective-permute-start.2 = (bf16[64,384]{1,0:T(8,128)(2,1)S(1)}, bf16[64,384]{1,0:T(8,128)(2,1)S(1)}, u32[]{:S(2)}, u32[]{:S(2)}) collective-permute-start(bf16[64,384]{1,0:T(8,128)(2,1)S(1)} %maximum_select_fusion.5), channel_id=1, source_target_pairs={{0,4},{1,5},{2,6},{3,7},{4,0},{5,1},{6,2},{7,3},{8,12},{9,13},{10,... | collective-permute-start | bytes 147464 | tf_op jit(solution)/shard_map/ppermute | solution.py:41
  281.0 59.4 %copy-start.1 = (bf16[4096,384]{1,0:T(8,128)(2,1)S(1)}, bf16[4096,384]{1,0:T(8,128)(2,1)}, u32[]{:S(2)}) copy-start(bf16[4096,384]{1,0:T(8,128)(2,1)} %param.5) | copy-start | bytes 9437188
  326.1 3.6 collective-permute-start.3
  329.7 10.6 %collective-permute-start.4 = (bf16[256,384]{1,0:T(8,128)(2,1)S(1)}, bf16[256,384]{1,0:T(8,128)(2,1)}, u32[]{:S(2)}, u32[]{:S(2)}) collective-permute-start(bf16[256,384]{1,0:T(8,128)(2,1)S(1)} %maximum_select_fusion.1), channel_id=1, source_target_pairs={{0,16},{1,17},{2,18},{3,19},{4,20},{5,21},{6,22},{7,23},{8,24},{9,... | collective-permute-start | bytes 589832 | tf_op jit(solution)/shard_map/ppermute | solution.py:41
  407.4 9.3 %copy-start.4 = (f32[4096]{0:T(1024)S(1)}, f32[4096]{0:T(1024)}, u32[]{:S(2)}) copy-start(f32[4096]{0:T(1024)} %copy-done.3) | copy-start | bytes 49156
  414.7 2.0 copy-start.2
  420.1 272.8 %reduce-scatter.5.cloned.1.call-start = ((), (), s32[]{:S(2)}) async-start(), calls=%async_computation.3 | async-start | bytes 7077888 | tf_op jit(solution)/shard_map/reduce_scatter | solution.py:79
Sparse Core Ops, SparseCore 0:
  420.2 221.5 reduce-scatter.2
  644.9 47.8 reduce-scatter.4
